TPU v7x, 128 devices: a whole 4x4x4 slice. The times are simulated.
128 devices in a mesh: group: 4 (over z_lo, core), dp: 2 (over z_hi), tensor: 16 (over x, y).
Axes of the slice: x: 4, y: 4, z: 4 (z_hi: 2, z_lo: 2; z = z_hi * 2 + z_lo), core: 2. Of those that a mesh axis runs over, the one named last changes fastest.
Arguments:
- tokens: bfloat16 [2048, 8, 2048], P('tensor', ('group', 'dp')), may hold values from -6 to 6
- cotangent: bfloat16 [2048, 8, 2048], P('tensor', ('group', 'dp')), may hold values from -6 to 6
- lengths: int32 [8], replicated, may hold values from 1 to 2048, 9830 in all
- ln1_gain: float32 [2048], replicated, may hold values from 0.25 to 1.75
- ln1_bias: float32 [2048], replicated, may hold values from -1.75 to 1.75
- w_qkv: bfloat16 [2048, 3, 16, 128], P(None, None, 'tensor'), may hold values from -0.125 to 0.125
- b_qv: float32 [2, 2048], P(None, 'tensor'), may hold values from -1.75 to 1.75
- w_o: bfloat16 [16, 128, 2048], P('tensor'), may hold values from -0.75 to 0.75
- b_o: float32 [2048], replicated, may hold values from -1.75 to 1.75
- ln2_gain: float32 [2048], replicated, may hold values from 0.25 to 1.75
- ln2_bias: float32 [2048], replicated, may hold values from -1.75 to 1.75
- w_in: bfloat16 [2048, 8192], P(None, 'tensor'), may hold values from -0.125 to 0.125
- b_in: float32 [8192], P('tensor'), may hold values from -1.75 to 1.75
- w_out: bfloat16 [8192, 2048], P('tensor'), may hold values from -0.0625 to 0.0625
- b_out: float32 [2048], replicated, may hold values from -1.75 to 1.75
Outputs:
- output: bfloat16 [2048, 8, 2048], P('tensor', ('group', 'dp'))
- input_grad: bfloat16 [2048, 8, 2048], P('tensor', ('group', 'dp'))
- d_ln1_gain: float32 [2048], P(('group', 'dp', 'tensor'))
- d_ln1_bias: float32 [2048], P(('group', 'dp', 'tensor'))
- d_w_qkv: float32 [2048, 3, 16, 128], P(('group', 'dp'), None, 'tensor')
- d_b_qv: float32 [2, 2048], P(None, ('group', 'dp', 'tensor'))
- d_w_o: float32 [16, 128, 2048], P('tensor', None, ('group', 'dp'))
- d_b_o: float32 [2048], P(('group', 'dp', 'tensor'))
- d_ln2_gain: float32 [2048], P(('group', 'dp', 'tensor'))
- d_ln2_bias: float32 [2048], P(('group', 'dp', 'tensor'))
- d_w_in: float32 [2048, 8192], P(('group', 'dp'), 'tensor')
- d_b_in: float32 [8192], P(('group', 'dp', 'tensor'))
- d_w_out: float32 [8192, 2048], P('tensor', ('group', 'dp'))
- d_b_out: float32 [2048], P(('group', 'dp', 'tensor'))
Inputs may be any that keep to these rules, and one draw needn't show every extreme that they name: The true lengths of the 8 sequences sum to 9830.
All inputs are finite; a program needn't handle non-finite values.
Results may differ from a plain program's by a relative error of at most 0.02.
Values may be sent and summed in bfloat16 or wider, within the bound.
No kernel may reach another device: no remote copies, remote signals or barrier semaphores. Data moves between devices by JAX's collectives and lax.ppermute only.
A program may use at most 192 MiB of HBM per device.

v0:
```python
from functools import partial
import math
import jax
import jax.numpy as jnp
from jax import lax
from jax.sharding import PartitionSpec as P

EPS = 1e-05
NEGATIVE = -1e30


def layer_norm(value, gain, shift):
    mean = jnp.mean(value, axis=-1, keepdims=True)
    centred = value - mean
    spread = jnp.mean(centred * centred, axis=-1, keepdims=True)
    return centred * lax.rsqrt(spread + EPS) * gain + shift


def gelu_tanh(value):
    return jax.nn.gelu(value, approximate=True)


def block_scores(rows_query, key_rows, first, length, score_scale):
    count = rows_query.shape[0]
    key_pos = jnp.arange(key_rows.shape[0], dtype=jnp.int32)
    query_pos = first + jnp.arange(count, dtype=jnp.int32)
    valid = (key_pos[None, :] <= query_pos[:, None]) & (key_pos[None, :] < length)
    scores = (
        lax.dot_general(
            rows_query, key_rows, (((1,), (1,)), ((), ())), preferred_element_type=jnp.float32
        )
        * score_scale
    )
    return (jnp.where(valid, scores, NEGATIVE), valid)


def attend_forward(item, block_rows, score_scale):
    query, key_rows, value_rows, length = item
    outputs = []
    log_parts = []
    for first in range(0, query.shape[0], block_rows):
        rows_query = query[first : first + block_rows]
        scores, valid = block_scores(rows_query, key_rows, first, length, score_scale)
        peak = jnp.max(scores, axis=-1, keepdims=True)
        expo = jnp.exp(scores - peak)
        weight_sum = jnp.sum(expo, axis=-1, keepdims=True)
        probs = (expo / weight_sum).astype(jnp.bfloat16)
        outputs.append(
            jnp.dot(probs, value_rows, preferred_element_type=jnp.float32).astype(jnp.bfloat16)
        )
        log_parts.append((peak + jnp.log(weight_sum))[:, 0])
    return (jnp.concatenate(outputs, 0), jnp.concatenate(log_parts, 0))


def attend_backward(item, block_rows, score_scale):
    query, key_rows, value_rows, length, grad_out, log_sums = item
    key_grad = jnp.zeros(key_rows.shape, jnp.float32)
    value_grad = jnp.zeros(value_rows.shape, jnp.float32)
    query_parts = []
    for first in range(0, query.shape[0], block_rows):
        rows_query = query[first : first + block_rows]
        scores, valid = block_scores(rows_query, key_rows, first, length, score_scale)
        probs = jnp.where(valid, jnp.exp(scores - log_sums[first : first + block_rows, None]), 0.0)
        grad_rows = grad_out[first : first + block_rows]
        probs_grad = lax.dot_general(
            grad_rows, value_rows, (((1,), (1,)), ((), ())), preferred_element_type=jnp.float32
        )
        inner = jnp.sum(probs * probs_grad, axis=-1, keepdims=True)
        score_grad = (probs * (probs_grad - inner)).astype(jnp.bfloat16)
        query_parts.append(
            jnp.dot(score_grad, key_rows, preferred_element_type=jnp.float32) * score_scale
        )
        key_grad = (
            key_grad
            + lax.dot_general(
                score_grad, rows_query, (((0,), (0,)), ((), ())), preferred_element_type=jnp.float32
            )
            * score_scale
        )
        value_grad = value_grad + lax.dot_general(
            probs.astype(jnp.bfloat16),
            grad_rows,
            (((0,), (0,)), ((), ())),
            preferred_element_type=jnp.float32,
        )
    return (
        jnp.concatenate(query_parts, 0).astype(jnp.bfloat16),
        key_grad.astype(jnp.bfloat16),
        value_grad.astype(jnp.bfloat16),
    )


def shards(
    tokens,
    cotangent,
    lengths,
    ln1_gain,
    ln1_bias,
    w_qkv,
    b_qv,
    w_o,
    b_o,
    ln2_gain,
    ln2_bias,
    w_in,
    b_in,
    w_out,
    b_out,
):
    row_count, seq_count, model_width = tokens.shape
    tensor_count = lax.axis_size("tensor")
    tensor_rank = lax.axis_index("tensor")
    seq_total = row_count * tensor_count
    local_heads = w_qkv.shape[2]
    head_size = w_qkv.shape[3]
    local_width = local_heads * head_size
    hidden = w_in.shape[1]
    block_rows = min(512, seq_total)
    score_scale = 1.0 / math.sqrt(head_size)
    group_count = lax.axis_size("group")
    group_rank = lax.axis_index("group")
    member = group_rank * lax.axis_size("dp") + lax.axis_index("dp")
    seq_lengths = lax.dynamic_slice_in_dim(lengths, member * seq_count, seq_count, 0)
    group_totals = jnp.sum(lengths.reshape(group_count, -1), axis=1).astype(jnp.float32)
    factor = (
        group_count
        * lax.dynamic_index_in_dim(group_totals, group_rank, 0, keepdims=False)
        / jnp.sum(group_totals)
    )
    inputs = tokens.astype(jnp.float32)
    normed_low = layer_norm(inputs, ln1_gain, ln1_bias).astype(jnp.bfloat16)
    normed_full = lax.all_gather(normed_low, "tensor", axis=0, tiled=True)
    joint_weight = w_qkv.reshape(model_width, 3 * local_width)
    projected = jnp.dot(
        normed_full.reshape(seq_total * seq_count, model_width),
        joint_weight,
        preferred_element_type=jnp.float32,
    )
    projected = projected.reshape(seq_total, seq_count, 3, local_width)
    query = (projected[:, :, 0] + b_qv[0]).astype(jnp.bfloat16)
    keys = projected[:, :, 1].astype(jnp.bfloat16)
    values = (projected[:, :, 2] + b_qv[1]).astype(jnp.bfloat16)

    def per_item(array):
        shaped = array.reshape(seq_total, seq_count, local_heads, head_size)
        return jnp.transpose(shaped, (1, 2, 0, 3)).reshape(
            seq_count * local_heads, seq_total, head_size
        )

    def per_row(array):
        shaped = array.reshape(seq_count, local_heads, seq_total, head_size)
        return jnp.transpose(shaped, (2, 0, 1, 3)).reshape(seq_total, seq_count, local_width)

    query_items = per_item(query)
    key_items = per_item(keys)
    value_items = per_item(values)
    item_lengths = jnp.repeat(seq_lengths, local_heads)
    heads_out, log_sums = lax.map(
        partial(attend_forward, block_rows=block_rows, score_scale=score_scale),
        (query_items, key_items, value_items, item_lengths),
    )
    attended = per_row(heads_out)
    out_weight = w_o.reshape(local_width, model_width)
    piece = attended
    attention = (
        lax.psum_scatter(
            jnp.einsum("rse,ed->rsd", piece, out_weight, preferred_element_type=jnp.float32),
            "tensor",
            scatter_dimension=0,
            tiled=True,
        )
        + b_o
    )
    middle = inputs + attention
    second_low = layer_norm(middle, ln2_gain, ln2_bias).astype(jnp.bfloat16)
    second_full = lax.all_gather(second_low, "tensor", axis=0, tiled=True)
    pre_act = (
        jnp.dot(
            second_full.reshape(seq_total * seq_count, model_width),
            w_in,
            preferred_element_type=jnp.float32,
        )
        + b_in
    )
    activated = gelu_tanh(pre_act).astype(jnp.bfloat16).reshape(seq_total, seq_count, hidden)
    piece = activated
    feed = (
        lax.psum_scatter(
            jnp.einsum("rsf,fd->rsd", piece, w_out, preferred_element_type=jnp.float32).astype(
                jnp.bfloat16
            ),
            "tensor",
            scatter_dimension=0,
            tiled=True,
        ).astype(jnp.float32)
        + b_out
    )
    output = (middle + feed).astype(jnp.bfloat16)
    positions = tensor_rank * row_count + jnp.arange(row_count, dtype=jnp.int32)
    live = positions[:, None] < seq_lengths[None, :]
    upstream = jnp.where(live[:, :, None], cotangent, jnp.zeros_like(cotangent))
    piece = lax.all_gather(upstream, "tensor", axis=0, tiled=True)
    weight_grad = jnp.einsum("rsf,rsd->fd", activated, piece, preferred_element_type=jnp.float32)
    part = jnp.einsum("rsd,fd->rsf", piece, w_out, preferred_element_type=jnp.float32)
    act_grad = part
    grad_w_out = weight_grad
    gelu_back = jax.vjp(gelu_tanh, pre_act)[1]
    pre_low = gelu_back(act_grad.reshape(seq_total * seq_count, hidden))[0].astype(jnp.bfloat16)
    grad_b_in = jnp.sum(pre_low, axis=0, dtype=jnp.float32)
    grad_w_in = jnp.einsum(
        "rd,rf->df",
        second_full.reshape(seq_total * seq_count, model_width),
        pre_low,
        preferred_element_type=jnp.float32,
    )
    pre_rows = pre_low.reshape(seq_total, seq_count, hidden)
    piece = pre_rows
    second_grad = lax.psum_scatter(
        jnp.einsum("rsf,df->rsd", piece, w_in, preferred_element_type=jnp.float32),
        "tensor",
        scatter_dimension=0,
        tiled=True,
    )
    norm_two_back = jax.vjp(layer_norm, middle, ln2_gain, ln2_bias)[1]
    middle_part, grad_ln2_gain, grad_ln2_bias = norm_two_back(second_grad)
    middle_grad = upstream.astype(jnp.float32) + middle_part
    branch_low = middle_grad.astype(jnp.bfloat16)
    grad_b_o = jnp.sum(branch_low, axis=(0, 1), dtype=jnp.float32)
    grad_b_out = jnp.sum(upstream, axis=(0, 1), dtype=jnp.float32)
    piece = lax.all_gather(branch_low, "tensor", axis=0, tiled=True)
    weight_grad = jnp.einsum("rse,rsd->ed", attended, piece, preferred_element_type=jnp.float32)
    part = jnp.einsum("rsd,ed->rse", piece, out_weight, preferred_element_type=jnp.float32)
    head_items = per_item(part.astype(jnp.bfloat16))
    grads_query, grads_keys, grads_values = lax.map(
        partial(attend_backward, block_rows=block_rows, score_scale=score_scale),
        (query_items, key_items, value_items, item_lengths, head_items, log_sums),
    )
    joint_grad = jnp.stack(
        (per_row(grads_query), per_row(grads_keys), per_row(grads_values)), axis=2
    )
    grad_b_qv = jnp.sum(joint_grad[:, :, 0::2], axis=(0, 1), dtype=jnp.float32)
    joint_rows = joint_grad.reshape(seq_total, seq_count, 3 * local_width)
    grad_w_qkv = jnp.einsum(
        "rd,rc->dc",
        normed_full.reshape(seq_total * seq_count, model_width),
        joint_rows.reshape(seq_total * seq_count, 3 * local_width),
        preferred_element_type=jnp.float32,
    )
    piece = joint_rows
    normed_grad = lax.psum_scatter(
        jnp.einsum("rsc,dc->rsd", piece, joint_weight, preferred_element_type=jnp.float32).astype(
            jnp.bfloat16
        ),
        "tensor",
        scatter_dimension=0,
        tiled=True,
    ).astype(jnp.float32)
    norm_one_back = jax.vjp(layer_norm, inputs, ln1_gain, ln1_bias)[1]
    input_part, grad_ln1_gain, grad_ln1_bias = norm_one_back(normed_grad)
    input_grad = (middle_grad + input_part).astype(jnp.bfloat16)
    matrices = (
        grad_w_qkv.reshape(model_width, 3, local_heads, head_size) * factor,
        weight_grad.reshape(local_heads, head_size, model_width) * factor,
        grad_w_in * factor,
        grad_w_out * factor,
    )
    summed = (
        lax.psum_scatter(
            matrices[0].astype(jnp.bfloat16), ("group", "dp"), scatter_dimension=0, tiled=True
        ).astype(jnp.float32),
        lax.psum_scatter(
            matrices[1].astype(jnp.bfloat16), ("group", "dp"), scatter_dimension=2, tiled=True
        ).astype(jnp.float32),
        lax.psum_scatter(
            matrices[2].astype(jnp.bfloat16), ("group", "dp"), scatter_dimension=0, tiled=True
        ).astype(jnp.float32),
        lax.psum_scatter(
            matrices[3].astype(jnp.bfloat16), ("group", "dp"), scatter_dimension=1, tiled=True
        ).astype(jnp.float32),
    )
    in_full = lax.dynamic_update_slice_in_dim(
        jnp.zeros((hidden * tensor_count,), jnp.float32), grad_b_in, tensor_rank * hidden, 0
    )
    joint_full = lax.dynamic_update_slice_in_dim(
        jnp.zeros((2, local_width * tensor_count), jnp.float32),
        grad_b_qv,
        tensor_rank * local_width,
        1,
    )
    stacked = (
        jnp.concatenate(
            (
                jnp.stack(
                    (
                        grad_ln1_gain,
                        grad_ln1_bias,
                        grad_b_o,
                        grad_ln2_gain,
                        grad_ln2_bias,
                        grad_b_out,
                    )
                ),
                joint_full,
            ),
            0,
        )
        * factor
    )
    vector_sums, in_sums = (
        lax.psum_scatter(stacked, ("group", "dp", "tensor"), scatter_dimension=1, tiled=True),
        lax.psum_scatter(
            in_full * factor, ("group", "dp", "tensor"), scatter_dimension=0, tiled=True
        ),
    )
    return (
        output,
        input_grad,
        vector_sums[0],
        vector_sums[1],
        summed[0],
        vector_sums[6:8],
        summed[1],
        vector_sums[2],
        vector_sums[3],
        vector_sums[4],
        summed[2],
        in_sums,
        summed[3],
        vector_sums[5],
    )


def solution(mesh):
    in_specs = (
        P("tensor", ("group", "dp"), None),
        P("tensor", ("group", "dp"), None),
        P(),
        P(),
        P(),
        P(None, None, "tensor", None),
        P(None, "tensor"),
        P("tensor", None, None),
        P(),
        P(),
        P(),
        P(None, "tensor"),
        P("tensor"),
        P("tensor", None),
        P(),
    )
    out_specs = (
        P("tensor", ("group", "dp"), None),
        P("tensor", ("group", "dp"), None),
        P(("group", "dp", "tensor")),
        P(("group", "dp", "tensor")),
        P(("group", "dp"), None, "tensor", None),
        P(None, ("group", "dp", "tensor")),
        P("tensor", None, ("group", "dp")),
        P(("group", "dp", "tensor")),
        P(("group", "dp", "tensor")),
        P(("group", "dp", "tensor")),
        P(("group", "dp"), "tensor"),
        P(("group", "dp", "tensor")),
        P("tensor", ("group", "dp")),
        P(("group", "dp", "tensor")),
    )
    return jax.shard_map(shards, mesh=mesh, in_specs=in_specs, out_specs=out_specs, check_vma=False)
```

profile of v0, /device:TPU:96, one launch (start us, length us, event | category | flops | bytes accessed | tf_op | source)
XLA Modules:
  0.0 1723.6 jit_solution(11324964571885417214)
XLA Ops:
  10.5 2.3 fusion.80
  12.8 2.6 copy.51
  16.8 68.1 %all-gather.5.cloned.1.call-done = bf16[2048,1,2048]{2,0,1:T(8,128)(2,1)} async-done(((bf16[128,1,2048]{2,0,1:T(8,128)(2,1)}), bf16[2048,1,2048]{2,0,1:T(8,128)(2,1)}) %all-gather.5.cloned.1.call-update) | async-done | bytes 8388624 | tf_op jit(solution)/shard_map/all_gather | solution.py:132
  84.8 7.4 fusion.31
  93.6 3.6 fusion.113
  97.1 3.9 fusion.116
  101.0 4.0 online-softmax.3
  106.0 5.1 fusion.115
  111.1 4.0 online-softmax.2
  116.1 5.1 fusion.114
  121.1 4.0 online-softmax.1
  126.2 4.4 online-softmax
  132.2 8.1 convolution_bitcast_fusion.1
  140.4 110.3 %reduce-scatter.12.cloned.1.call-done = f32[128,1,2048]{2,0,1:T(8,128)} async-done(((f32[2048,1,2048]{2,0,1:T(8,128)}), f32[128,1,2048]{2,0,1:T(8,128)}) %reduce-scatter.12.cloned.1.call-update) | async-done | bytes 1048592 | tf_op jit(solution)/shard_map/reduce_scatter | solution.py:166
  256.1 2.6 convert_reduce_fusion.4
  258.8 67.0 %all-gather.7.cloned.1.call-done = bf16[2048,1,2048]{2,0,1:T(8,128)(2,1)} async-done(((bf16[128,1,2048]{2,0,1:T(8,128)(2,1)}), bf16[2048,1,2048]{2,0,1:T(8,128)(2,1)}) %all-gather.7.cloned.1.call-update) | async-done | bytes 8388624 | tf_op jit(solution)/shard_map/all_gather | solution.py:176
  325.7 10.5 fusion.10
  336.2 62.4 %all-gather.9.cloned.1.call-done = bf16[2048,1,2048]{2,0,1:T(8,128)(2,1)} async-done(((bf16[128,1,2048]{2,0,1:T(8,128)(2,1)}), bf16[2048,1,2048]{2,0,1:T(8,128)(2,1)}) %all-gather.9.cloned.1.call-update) | async-done | bytes 8388624 | tf_op jit(solution)/shard_map/all_gather | solution.py:202
  398.7 12.4 convert_reduce_fusion
  412.5 8.2 convolution_bitcast_fusion
  420.8 10.3 convert_bitcast_fusion.1
  431.2 99.9 %reduce-scatter.16.cloned.1.call-done = f32[128,1,2048]{2,0,1:T(8,128)} async-done(((f32[2048,1,2048]{2,0,1:T(8,128)}), f32[128,1,2048]{2,0,1:T(8,128)}) %reduce-scatter.16.cloned.1.call-update) | async-done | bytes 1048592 | tf_op jit(solution)/shard_map/reduce_scatter | solution.py:218
  531.1 2.2 multiply_reduce_fusion.4
  533.3 85.7 %reduce-scatter.14.cloned.1.call-done = bf16[128,1,2048]{2,0,1:T(8,128)(2,1)} async-done(((bf16[2048,1,2048]{2,0,1:T(8,128)(2,1)}), bf16[128,1,2048]{2,0,1:T(8,128)(2,1)}) %reduce-scatter.14.cloned.1.call-update) | async-done | bytes 524304 | tf_op jit(solution)/shard_map/reduce_scatter | solution.py:188
  619.0 2.5 fusion.110
  625.8 11.3 multiply_convert_fusion
  637.2 3.1 exponential_reduce_fusion
  645.5 9.6 multiply_convert_fusion.1
  655.6 37.3 %all-gather.11.cloned.1.call-done = bf16[2048,1,2048]{2,0,1:T(8,128)(2,1)} async-done(((bf16[128,1,2048]{2,0,1:T(8,128)(2,1)}), bf16[2048,1,2048]{2,0,1:T(8,128)(2,1)}) %all-gather.11.cloned.1.call-update) | async-done | bytes 8388624 | tf_op jit(solution)/shard_map/all_gather | solution.py:230
  692.9 5.9 fusion.45
  698.8 2.8 fusion.97
  701.7 2.9 fusion.100
  704.6 2.7 fusion.103
  708.0 9.5 multiply_reduce_fusion
  717.5 4.5 multiply_convert_fusion.3
  722.1 9.5 multiply_convert_fusion.2
  731.6 2.1 fusion.75
  733.7 3.3 fusion.77
  747.2 2.8 fusion.56
  750.0 2.3 fusion.53
  755.2 8.3 fusion.38
  763.6 9.7 convert_bitcast_fusion
  774.1 75.9 %all-reduce = f32[8192]{0:T(1024)S(1)} all-reduce(f32[8192]{0:T(1024)S(1)} %broadcast_multiply_fusion.1), channel_id=10, replica_groups=mesh['group'=4,'dp'=2,'tensor'=16] {'group','dp','tensor'}, use_global_device_ids=true, to_apply=%region_38.39.clone | all-reduce | flops 8192 | bytes 65536
  857.0 45.5 %reduce-scatter.20.cloned.1.call-done = bf16[256,3,1,128]{3,0,1,2:T(8,128)(2,1)} async-done(((bf16[2048,3,1,128]{3,0,1,2:T(8,128)(2,1)}), bf16[256,3,1,128]{3,0,1,2:T(8,128)(2,1)}) %reduce-scatter.20.cloned.1.call-update) | async-done | bytes 196624 | tf_op jit(solution)/shard_map/reduce_scatter | solution.py:268
  902.5 2.0 copy.62
  904.5 90.2 %reduce-scatter.18.cloned.1.call-done = bf16[128,1,2048]{2,0,1:T(8,128)(2,1)} async-done(((bf16[2048,1,2048]{2,0,1:T(8,128)(2,1)}), bf16[128,1,2048]{2,0,1:T(8,128)(2,1)}) %reduce-scatter.18.cloned.1.call-update) | async-done | bytes 524304 | tf_op jit(solution)/shard_map/reduce_scatter | solution.py:250
  999.2 2.7 add_convert_fusion
  1002.0 709.0 %reduce-scatter.28.cloned.1.call-done = f32[16,8]{1,0:T(8,128)} async-done(((f32[2048,8]{1,0:T(8,128)}), f32[16,8]{1,0:T(8,128)}) %reduce-scatter.28.cloned.1.call-update) | async-done | bytes 528
  (255 shorter events, 57.8 us)
Async XLA Ops:
  7.2 391.5 %copy-start = (bf16[512,2048]{1,0:T(8,128)(2,1)S(1)}, bf16[512,2048]{1,0:T(8,128)(2,1)}, u32[]{:S(2)}) copy-start(bf16[512,2048]{1,0:T(8,128)(2,1)} %param.28) | copy-start | bytes 6291460
  7.2 77.6 %all-gather.5.cloned.1.call-start = ((), (), s32[]{:S(2)}) async-start(), calls=%async_computation.9 | async-start | bytes 8912896 | tf_op jit(solution)/shard_map/all_gather | solution.py:132
  9.9 82.3 %copy-start.68 = (f32[128]{0:T(128)}, f32[128]{0:T(128)S(1)}, u32[]{:S(2)}) copy-start(f32[128]{0:T(128)S(1)} %fusion.81) | copy-start | bytes 1540
  12.8 237.9 %reduce-scatter.12.cloned.1.call-start = ((), (), s32[]{:S(2)}) async-start(), calls=%async_computation.10 | async-start | bytes 17825792 | tf_op jit(solution)/shard_map/reduce_scatter | solution.py:166
  16.0 100.0 %copy-start.35 = (s32[512]{0:T(512)}, s32[512]{0:T(512)S(1)}, u32[]{:S(2)}) copy-start(s32[512]{0:T(512)S(1)} %iota_add_fusion.2) | copy-start | bytes 6148
  16.0 89.9 %copy-start.33 = (s32[512]{0:T(512)}, s32[512]{0:T(512)S(1)}, u32[]{:S(2)}) copy-start(s32[512]{0:T(512)S(1)} %iota_add_fusion.1) | copy-start | bytes 6148
  16.7 75.6 %copy-start.56 = (f32[128]{0:T(128)}, f32[128]{0:T(128)S(1)}, u32[]{:S(2)}) copy-start(f32[128]{0:T(128)S(1)} %get-tuple-element.136) | copy-start | bytes 1540
  92.3 23.7 %copy-start.17 = (bf16[2048,1,128]{2,0,1:T(8,128)(2,1)}, bf16[2048,1,128]{2,0,1:T(8,128)(2,1)S(1)}, u32[]{:S(2)}) copy-start(bf16[2048,1,128]{2,0,1:T(8,128)(2,1)S(1)} %fusion.85) | copy-start | bytes 1572868
  140.3 113.3 %copy-start.29 = (f32[2048]{0:T(1024)S(1)}, f32[2048]{0:T(1024)}, u32[]{:S(2)}) copy-start(f32[2048]{0:T(1024)} %param.24) | copy-start | bytes 24580
  140.3 185.4 %all-gather.7.cloned.1.call-start = ((), (), s32[]{:S(2)}) async-start(), calls=%async_computation.11 | async-start | bytes 8912896 | tf_op jit(solution)/shard_map/all_gather | solution.py:176
  255.3 143.3 %all-gather.9.cloned.1.call-start = ((), (), s32[]{:S(2)}) async-start(), calls=%async_computation.13 | async-start | bytes 8912896 | tf_op jit(solution)/shard_map/all_gather | solution.py:202
  258.7 272.4 %reduce-scatter.16.cloned.1.call-start = ((), (), s32[]{:S(2)}) async-start(), calls=%async_computation.14 | async-start | bytes 17825792 | tf_op jit(solution)/shard_map/reduce_scatter | solution.py:218
  398.7 13.8 copy-start.70
  420.7 198.3 %reduce-scatter.14.cloned.1.call-start = ((), (), s32[]{:S(2)}) async-start(), calls=%async_computation.12 | async-start | bytes 8912896 | tf_op jit(solution)/shard_map/reduce_scatter | solution.py:188
  431.0 100.0 %copy-start.53 = (f32[128]{0:T(128)S(1)}, f32[128]{0:T(128)}, u32[]{:S(2)}) copy-start(f32[128]{0:T(128)} %copy-done.52) | copy-start | bytes 1540
  431.0 100.0 %copy-start.59 = (f32[128]{0:T(128)S(1)}, f32[128]{0:T(128)}, u32[]{:S(2)}) copy-start(f32[128]{0:T(128)} %copy-done.58) | copy-start | bytes 1540
  431.0 102.2 %copy-start.65 = (f32[128]{0:T(128)S(1)}, f32[128]{0:T(128)}, u32[]{:S(2)}) copy-start(f32[128]{0:T(128)} %copy-done.64) | copy-start | bytes 1540
  431.0 188.0 %copy-start.51 = (f32[2048]{0:T(1024)S(1)}, f32[2048]{0:T(1024)}, u32[]{:S(2)}) copy-start(f32[2048]{0:T(1024)} %param.29) | copy-start | bytes 24580
  431.1 190.5 %copy-start.15 = (bf16[128,1,2048]{2,0,1:T(8,128)(2,1)S(1)}, bf16[128,1,2048]{2,0,1:T(8,128)(2,1)}, u32[]{:S(2)}) copy-start(bf16[128,1,2048]{2,0,1:T(8,128)(2,1)} %get-tuple-element.119) | copy-start | bytes 1572868
  431.1 191.9 %copy-start.67 = (s32[8]{0:T(128)S(1)}, s32[8]{0:T(128)}, u32[]{:S(2)}) copy-start(s32[8]{0:T(128)} %param.17) | copy-start | bytes 100
  431.1 194.6 %copy-start.71 = (f32[512]{0:T(512)S(1)}, f32[512]{0:T(512)}, u32[]{:S(2)}) copy-start(f32[512]{0:T(512)} %param.27) | copy-start | bytes 6148
  431.1 261.8 %all-gather.11.cloned.1.call-start = ((), (), s32[]{:S(2)}) async-start(), calls=%async_computation.15 | async-start | bytes 8912896 | tf_op jit(solution)/shard_map/all_gather | solution.py:230
  621.6 15.5 copy-start.14
  621.6 15.5 copy-start.60
  622.7 227.9 %reduce-scatter.26.cloned.1.call-start = ((), (), s32[]{:S(2)}) async-start(), calls=%async_computation.20 | async-start | bytes 2359296 | tf_op jit(solution)/shard_map/reduce_scatter | solution.py:277
  625.7 11.4 copy-start.48
  637.1 215.3 %reduce-scatter.24.cloned.1.call-start = ((), (), s32[]{:S(2)}) async-start(), calls=%async_computation.19 | async-start | bytes 2359296 | tf_op jit(solution)/shard_map/reduce_scatter | solution.py:274
  641.4 76.1 %copy-start.39 = (f32[512]{0:T(512)}, f32[512]{0:T(512)S(1)}, u32[]{:S(2)}) copy-start(f32[512]{0:T(512)S(1)} %get-tuple-element.150) | copy-start | bytes 6148
  641.4 80.6 %copy-start.37 = (f32[512]{0:T(512)}, f32[512]{0:T(512)S(1)}, u32[]{:S(2)}) copy-start(f32[512]{0:T(512)S(1)} %get-tuple-element.149) | copy-start | bytes 6148
  644.2 77.9 %copy-start.41 = (f32[512]{0:T(512)}, f32[512]{0:T(512)S(1)}, u32[]{:S(2)}) copy-start(f32[512]{0:T(512)S(1)} %get-tuple-element.151) | copy-start | bytes 6148
  644.2 77.9 %copy-start.43 = (f32[512]{0:T(512)}, f32[512]{0:T(512)S(1)}, u32[]{:S(2)}) copy-start(f32[512]{0:T(512)S(1)} %get-tuple-element.152) | copy-start | bytes 6148
  645.5 47.4 %copy-start.24 = (bf16[1,128,2048]{2,1,0:T(8,128)(2,1)S(1)}, bf16[1,128,2048]{2,1,0:T(8,128)(2,1)}, u32[]{:S(2)}) copy-start(bf16[1,128,2048]{2,1,0:T(8,128)(2,1)} %param.22) | copy-start | bytes 1572868
  655.2 200.2 %reduce-scatter.22.cloned.1.call-start = ((), (), s32[]{:S(2)}) async-start(), calls=%async_computation.18 | async-start | bytes 589824 | tf_op jit(solution)/shard_map/reduce_scatter | solution.py:271
  692.9 14.3 copy-start.8
  752.4 150.2 %reduce-scatter.20.cloned.1.call-start = ((), (), s32[]{:S(2)}) async-start(), calls=%async_computation.17 | async-start | bytes 1769472 | tf_op jit(solution)/shard_map/reduce_scatter | solution.py:268
  763.6 231.1 %reduce-scatter.18.cloned.1.call-start = ((), (), s32[]{:S(2)}) async-start(), calls=%async_computation.16 | async-start | bytes 8912896 | tf_op jit(solution)/shard_map/reduce_scatter | solution.py:250
  773.3 221.4 %copy-start.9 = (bf16[128,1,2048]{2,0,1:T(8,128)(2,1)S(1)}, bf16[128,1,2048]{2,0,1:T(8,128)(2,1)}, u32[]{:S(2)}) copy-start(bf16[128,1,2048]{2,0,1:T(8,128)(2,1)} %param.15) | copy-start | bytes 1572868
  773.3 221.4 %copy-start.28 = (f32[2048]{0:T(1024)S(1)}, f32[2048]{0:T(1024)}, u32[]{:S(2)}) copy-start(f32[2048]{0:T(1024)} %param.18) | copy-start | bytes 24580
  773.3 221.4 %copy-start.46 = (f32[128]{0:T(128)S(1)}, f32[128]{0:T(128)}, u32[]{:S(2)}) copy-start(f32[128]{0:T(128)} %copy-done.45) | copy-start | bytes 1540
  773.3 222.8 %copy-start.69 = (f32[128]{0:T(128)S(1)}, f32[128]{0:T(128)}, u32[]{:S(2)}) copy-start(f32[128]{0:T(128)} %copy-done.68) | copy-start | bytes 1540
  773.3 222.8 %copy-start.55 = (f32[128]{0:T(128)S(1)}, f32[128]{0:T(128)}, u32[]{:S(2)}) copy-start(f32[128]{0:T(128)} %copy-done.54) | copy-start | bytes 1540
  773.3 224.4 %copy-start.30 = (f32[2048]{0:T(1024)S(1)}, f32[2048]{0:T(1024)}, u32[]{:S(2)}) copy-start(f32[2048]{0:T(1024)} %get-tuple-element.118) | copy-start | bytes 24580
  773.3 224.4 %copy-start.31 = (f32[2048]{0:T(1024)S(1)}, f32[2048]{0:T(1024)}, u32[]{:S(2)}) copy-start(f32[2048]{0:T(1024)} %get-tuple-element.107) | copy-start | bytes 24580
  773.4 224.4 %copy-start.32 = (f32[2048]{0:T(1024)S(1)}, f32[2048]{0:T(1024)}, u32[]{:S(2)}) copy-start(f32[2048]{0:T(1024)} %get-tuple-element.111) | copy-start | bytes 24580
  773.4 225.9 %copy-start.16 = (bf16[128,1,2048]{2,0,1:T(8,128)(2,1)S(1)}, bf16[128,1,2048]{2,0,1:T(8,128)(2,1)}, u32[]{:S(2)}) copy-start(bf16[128,1,2048]{2,0,1:T(8,128)(2,1)} %get-tuple-element.119) | copy-start | bytes 1572868
  773.4 225.9 %copy-start.61 = (f32[128]{0:T(128)S(1)}, f32[128]{0:T(128)}, u32[]{:S(2)}) copy-start(f32[128]{0:T(128)} %copy-done.60) | copy-start | bytes 1540
  773.4 937.6 %reduce-scatter.28.cloned.1.call-start = ((), (), s32[]{:S(2)}) async-start(), calls=%async_computation.21 | async-start | bytes 1056768
  855.4 861.5 %copy-start.1 = (bf16[512,2048]{1,0:T(8,128)(2,1)S(1)}, bf16[512,2048]{1,0:T(8,128)(2,1)}, u32[]{:S(2)}) copy-start(bf16[512,2048]{1,0:T(8,128)(2,1)} %param.28) | copy-start | bytes 6291460
  (41 other events, 150.4 us)
Sparse Core Ops, SparseCore 0:
  12.9 71.8 all-gather.4
  140.5 110.1 reduce-scatter.11
  255.5 70.2 all-gather.6
  328.3 70.3 all-gather.8
  420.8 110.1 reduce-scatter.15
  534.3 84.6 reduce-scatter.13
  622.8 70.0 all-gather.10
  695.3 56.2 reduce-scatter.25
  754.1 60.7 reduce-scatter.23
  817.0 38.2 reduce-scatter.21
  857.9 44.5 reduce-scatter.19
  906.2 88.4 reduce-scatter.17
  999.3 711.5 reduce-scatter.27
where the time goes:
time: 1730 us; the launch traced here: 1720 us
  waiting for transfers between devices  1380 us (80%)
  matrix products  158 us (9%)
  blocking collectives  75.9 us (4%)
  other arithmetic  57.2 us (3%)
  local copies, waits for them, and re-layouts  22.4 us (1%)
    unnamed x14, waiting for transfers between devices  709 us
    reduce_scatter x1, waiting for transfers between devices, shards(): lax.psum_scatter(jnp.einsum('rse,ed->rsd', piece, out_weight, preferred_e...  110 us
    reduce_scatter x1, waiting for transfers between devices, shards(): lax.psum_scatter(jnp.einsum('rsf,df->rsd', piece, w_in, preferred_element...  99.9 us
    reduce_scatter x1, waiting for transfers between devices, shards(): lax.psum_scatter(jnp.einsum('rsc,dc->rsd', piece, joint_weight, preferred...  90.2 us
    reduce_scatter x1, waiting for transfers between devices, shards(): lax.psum_scatter(jnp.einsum('rsf,fd->rsd', piece, w_out, preferred_elemen...  85.7 us
    unnamed x1, blocking collectives  75.9 us
    all_gather x1, waiting for transfers between devices, shards(): normed_full = lax.all_gather(normed_low, 'tensor', axis=0, tiled=True)  68.1 us
    all_gather x1, waiting for transfers between devices, shards(): second_full = lax.all_gather(second_low, 'tensor', axis=0, tiled=True)  67 us
  transfers between devices with their start and end apart: 13, of which 11 were waited for; matrix products, arithmetic and copies ran while one was open for 9% of the time, Pallas kernels for 0%

commit v1 on v0

--- a/solution.py
+++ b/solution.py
@@ -199,7 +199,9 @@
     positions = tensor_rank * row_count + jnp.arange(row_count, dtype=jnp.int32)
     live = positions[:, None] < seq_lengths[None, :]
     upstream = jnp.where(live[:, :, None], cotangent, jnp.zeros_like(cotangent))
-    piece = lax.all_gather(upstream, "tensor", axis=0, tiled=True)
+    piece = jnp.concatenate(
+        lax.all_to_all(jnp.stack([upstream] * lax.axis_size("tensor")), "tensor", 0, 0), axis=0
+    )
     weight_grad = jnp.einsum("rsf,rsd->fd", activated, piece, preferred_element_type=jnp.float32)
     part = jnp.einsum("rsd,fd->rsf", piece, w_out, preferred_element_type=jnp.float32)
     act_grad = part

time: 1730 us -> 1840 us (1.064)
  waiting for transfers between devices: 1380 us -> 1470 us
    all_gather x1, waiting for transfers between devices: 67 us -> 172 us  [shards(): second_full = lax.all_gather(second_low, 'tensor', axis=0, tiled=True)]
    all_gather x1 -> x0, waiting for transfers between devices: 62.4 us -> none  [shards(): piece = lax.all_gather(upstream, 'tensor', axis=0, tiled=True)]
    reduce_scatter x1, waiting for transfers between devices: 90.2 us -> 45 us  [shards(): lax.psum_scatter(jnp.einsum('rsc,dc->rsd', piece, joint_weight, preferred...]
    reduce_scatter x1, waiting for transfers between devices: 0.86 us -> 38.7 us  [shards(): lax.psum_scatter(matrices[1].astype(jnp.bfloat16), ('group', 'dp'), scatt...]
    reduce_scatter x1, waiting for transfers between devices: 0.01 us -> 27.6 us  [shards(): lax.psum_scatter(matrices[2].astype(jnp.bfloat16), ('group', 'dp'), scatt...]
    all_gather x1, waiting for transfers between devices: 37.3 us -> 61.5 us  [shards(): piece = lax.all_gather(branch_low, 'tensor', axis=0, tiled=True)]
    unnamed x14 -> x13, waiting for transfers between devices: 709 us -> 716 us
  transfers between devices with their start and end apart: 13 -> 13, of which waited for: 11 -> 11; matrix products, arithmetic and copies ran while one was open for 9% -> 5% of each run, Pallas kernels for 0% -> 0%
where the time goes in v1:
time: 1840 us; the launch traced here: 1830 us
  waiting for transfers between devices  1470 us (80%)
  matrix products  156 us (8%)
  blocking collectives  84.3 us (5%)
  other arithmetic  51.6 us (3%)
  local copies, waits for them, and re-layouts  25.8 us (1%)
    unnamed x13, waiting for transfers between devices  716 us
    all_gather x1, waiting for transfers between devices, shards(): second_full = lax.all_gather(second_low, 'tensor', axis=0, tiled=True)  172 us
    reduce_scatter x1, waiting for transfers between devices, shards(): lax.psum_scatter(jnp.einsum('rse,ed->rsd', piece, out_weight, preferred_e...  110 us
    reduce_scatter x1, waiting for transfers between devices, shards(): lax.psum_scatter(jnp.einsum('rsf,df->rsd', piece, w_in, preferred_element...  103 us
    reduce_scatter x1, waiting for transfers between devices, shards(): lax.psum_scatter(jnp.einsum('rsf,fd->rsd', piece, w_out, preferred_elemen...  86.3 us
    unnamed x1, blocking collectives  84.3 us
    all_gather x1, waiting for transfers between devices, shards(): normed_full = lax.all_gather(normed_low, 'tensor', axis=0, tiled=True)  68.1 us
    all_gather x1, waiting for transfers between devices, shards(): piece = lax.all_gather(branch_low, 'tensor', axis=0, tiled=True)  61.5 us
  transfers between devices with their start and end apart: 13, of which 11 were waited for; matrix products, arithmetic and copies ran while one was open for 5% of the time, Pallas kernels for 0%

profile of v1, /device:TPU:96, one launch (start us, length us, event | category | flops | bytes accessed | tf_op | source)
XLA Modules:
  0.0 1831.3 jit_solution(7939760736498513858)
XLA Ops:
  10.5 2.3 fusion.72
  12.8 2.6 copy.51
  16.7 68.1 %all-gather.4.cloned.1.call-done = bf16[2048,1,2048]{2,0,1:T(8,128)(2,1)} async-done(((bf16[128,1,2048]{2,0,1:T(8,128)(2,1)}), bf16[2048,1,2048]{2,0,1:T(8,128)(2,1)}) %all-gather.4.cloned.1.call-update) | async-done | bytes 8388624 | tf_op jit(solution)/shard_map/all_gather | solution.py:132
  84.8 7.4 fusion.25
  93.5 2.9 fusion.107
  96.5 3.3 fusion.110
  99.8 4.1 online-softmax.3
  104.8 4.5 fusion.109
  109.4 4.0 online-softmax.2
  114.3 4.6 fusion.108
  118.9 4.0 online-softmax.1
  123.9 4.2 online-softmax
  129.2 8.0 convolution_bitcast_fusion.1
  137.3 110.2 %reduce-scatter.12.cloned.1.call-done = f32[128,1,2048]{2,0,1:T(8,128)} async-done(((f32[2048,1,2048]{2,0,1:T(8,128)}), f32[128,1,2048]{2,0,1:T(8,128)}) %reduce-scatter.12.cloned.1.call-update) | async-done | bytes 1048592 | tf_op jit(solution)/shard_map/reduce_scatter | solution.py:166
  252.3 4.3 stack.16
  256.6 5.2 all-to-all-start
  261.9 171.9 %all-gather.6.cloned.1.call-done = bf16[2048,1,2048]{2,0,1:T(8,128)(2,1)} async-done(((bf16[128,1,2048]{2,0,1:T(8,128)(2,1)}), bf16[2048,1,2048]{2,0,1:T(8,128)(2,1)}) %all-gather.6.cloned.1.call-update) | async-done | bytes 8388624 | tf_op jit(solution)/shard_map/all_gather | solution.py:176
  433.8 10.5 fusion.6
  444.4 12.4 convert_reduce_fusion
  458.2 8.3 convolution_bitcast_fusion
  466.5 10.1 convert_bitcast_fusion.1
  476.7 102.6 %reduce-scatter.16.cloned.1.call-done = f32[128,1,2048]{2,0,1:T(8,128)} async-done(((f32[2048,1,2048]{2,0,1:T(8,128)}), f32[128,1,2048]{2,0,1:T(8,128)}) %reduce-scatter.16.cloned.1.call-update) | async-done | bytes 1048592 | tf_op jit(solution)/shard_map/reduce_scatter | solution.py:220
  581.0 86.3 %reduce-scatter.14.cloned.1.call-done = bf16[128,1,2048]{2,0,1:T(8,128)(2,1)} async-done(((bf16[2048,1,2048]{2,0,1:T(8,128)(2,1)}), bf16[128,1,2048]{2,0,1:T(8,128)(2,1)}) %reduce-scatter.14.cloned.1.call-update) | async-done | bytes 524304 | tf_op jit(solution)/shard_map/reduce_scatter | solution.py:188
  667.3 2.6 fusion.104
  672.1 3.0 exponential_reduce_fusion
  680.2 61.5 %all-gather.8.cloned.1.call-done = bf16[2048,1,2048]{2,0,1:T(8,128)(2,1)} async-done(((bf16[128,1,2048]{2,0,1:T(8,128)(2,1)}), bf16[2048,1,2048]{2,0,1:T(8,128)(2,1)}) %all-gather.8.cloned.1.call-update) | async-done | bytes 8388624 | tf_op jit(solution)/shard_map/all_gather | solution.py:232
  741.7 5.7 fusion.37
  747.5 2.7 fusion.89
  750.2 2.8 fusion.92
  753.0 2.8 fusion.95
  759.5 10.2 multiply_reduce_fusion
  769.7 9.4 multiply_convert_fusion.2
  779.1 2.0 fusion.70
  785.4 2.0 fusion.48
  787.6 2.2 multiply_convert_fusion.3
  796.0 9.7 convert_bitcast_fusion
  809.1 11.3 multiply_convert_fusion
  820.5 10.2 multiply_convert_fusion.1
  830.7 5.5 fusion.45
  836.5 8.4 fusion.30
  845.7 45.0 %reduce-scatter.18.cloned.1.call-done = bf16[128,1,2048]{2,0,1:T(8,128)(2,1)} async-done(((bf16[2048,1,2048]{2,0,1:T(8,128)(2,1)}), bf16[128,1,2048]{2,0,1:T(8,128)(2,1)}) %reduce-scatter.18.cloned.1.call-update) | async-done | bytes 524304 | tf_op jit(solution)/shard_map/reduce_scatter | solution.py:252
  894.0 2.9 convert_reduce_fusion.4
  898.3 84.3 %all-reduce = f32[8192]{0:T(1024)S(1)} all-reduce(f32[8192]{0:T(1024)S(1)} %broadcast_multiply_fusion.1), channel_id=10, replica_groups=mesh['group'=4,'dp'=2,'tensor'=16] {'group','dp','tensor'}, use_global_device_ids=true, to_apply=%region_38.39.clone | all-reduce | flops 8192 | bytes 65536
  985.0 27.6 %reduce-scatter.24.cloned.1.call-done = bf16[256,512]{1,0:T(8,128)(2,1)} async-done(((bf16[2048,512]{1,0:T(8,128)(2,1)}), bf16[256,512]{1,0:T(8,128)(2,1)}) %reduce-scatter.24.cloned.1.call-update) | async-done | bytes 262160 | tf_op jit(solution)/shard_map/reduce_scatter | solution.py:276
  1014.4 38.7 %reduce-scatter.22.cloned.1.call-done = bf16[1,128,256]{2,1,0:T(8,128)(2,1)} async-done(((bf16[1,128,2048]{2,1,0:T(8,128)(2,1)}), bf16[1,128,256]{2,1,0:T(8,128)(2,1)}) %reduce-scatter.22.cloned.1.call-update) | async-done | bytes 65552 | tf_op jit(solution)/shard_map/reduce_scatter | solution.py:273
  1054.6 45.8 %reduce-scatter.20.cloned.1.call-done = bf16[256,3,1,128]{3,0,1,2:T(8,128)(2,1)} async-done(((bf16[2048,3,1,128]{3,0,1,2:T(8,128)(2,1)}), bf16[256,3,1,128]{3,0,1,2:T(8,128)(2,1)}) %reduce-scatter.20.cloned.1.call-update) | async-done | bytes 196624 | tf_op jit(solution)/shard_map/reduce_scatter | solution.py:270
  1100.4 2.0 copy.62
  1102.4 716.0 %reduce-scatter.28.cloned.1.call-done = f32[16,8]{1,0:T(8,128)} async-done(((f32[2048,8]{1,0:T(8,128)}), f32[16,8]{1,0:T(8,128)}) %reduce-scatter.28.cloned.1.call-update) | async-done | bytes 528
  (238 shorter events, 58.4 us)
Async XLA Ops:
  7.2 437.2 %copy-start = (bf16[512,2048]{1,0:T(8,128)(2,1)S(1)}, bf16[512,2048]{1,0:T(8,128)(2,1)}, u32[]{:S(2)}) copy-start(bf16[512,2048]{1,0:T(8,128)(2,1)} %param.28) | copy-start | bytes 6291460
  7.2 77.6 %all-gather.4.cloned.1.call-start = ((), (), s32[]{:S(2)}) async-start(), calls=%async_computation.10 | async-start | bytes 8912896 | tf_op jit(solution)/shard_map/all_gather | solution.py:132
  9.9 82.3 %copy-start.61 = (f32[128]{0:T(128)}, f32[128]{0:T(128)S(1)}, u32[]{:S(2)}) copy-start(f32[128]{0:T(128)S(1)} %fusion.73) | copy-start | bytes 1540
  12.8 234.8 %reduce-scatter.12.cloned.1.call-start = ((), (), s32[]{:S(2)}) async-start(), calls=%async_computation.11 | async-start | bytes 17825792 | tf_op jit(solution)/shard_map/reduce_scatter | solution.py:166
  16.0 741.7 %copy-start.36 = (s32[512]{0:T(512)}, s32[512]{0:T(512)S(1)}, u32[]{:S(2)}) copy-start(s32[512]{0:T(512)S(1)} %iota_add_fusion.2) | copy-start | bytes 6148
  16.0 741.7 %copy-start.34 = (s32[512]{0:T(512)}, s32[512]{0:T(512)S(1)}, u32[]{:S(2)}) copy-start(s32[512]{0:T(512)S(1)} %iota_add_fusion) | copy-start | bytes 6148
  92.3 22.0 %copy-start.17 = (bf16[2048,1,128]{2,0,1:T(8,128)(2,1)}, bf16[2048,1,128]{2,0,1:T(8,128)(2,1)S(1)}, u32[]{:S(2)}) copy-start(bf16[2048,1,128]{2,0,1:T(8,128)(2,1)S(1)} %fusion.77) | copy-start | bytes 1572868
  104.8 24.3 %copy-start.19 = (bf16[512,128]{1,0:T(8,128)(2,1)}, bf16[512,128]{1,0:T(8,128)(2,1)S(1)}, u32[]{:S(2)}) copy-start(bf16[512,128]{1,0:T(8,128)(2,1)S(1)} %convert_element_type.224) | copy-start | bytes 393220
  114.3 14.8 copy-start.21
  123.9 13.3 copy-start.23
  137.2 110.3 %copy-start.47 = (f32[2048]{0:T(1024)S(1)}, f32[2048]{0:T(1024)}, u32[]{:S(2)}) copy-start(f32[2048]{0:T(1024)} %param.23) | copy-start | bytes 24580
  137.2 112.2 %copy-start.32 = (f32[2048]{0:T(1024)S(1)}, f32[2048]{0:T(1024)}, u32[]{:S(2)}) copy-start(f32[2048]{0:T(1024)} %param.24) | copy-start | bytes 24580
  137.2 112.2 %copy-start.48 = (f32[2048]{0:T(1024)S(1)}, f32[2048]{0:T(1024)}, u32[]{:S(2)}) copy-start(f32[2048]{0:T(1024)} %param.25) | copy-start | bytes 24580
  137.3 296.6 %all-gather.6.cloned.1.call-start = ((), (), s32[]{:S(2)}) async-start(), calls=%async_computation.12 | async-start | bytes 8912896 | tf_op jit(solution)/shard_map/all_gather | solution.py:176
  251.2 418.7 %copy-start.53 = (pred[128]{0:T(512)(128)(4,1)}, pred[128]{0:T(512)(128)(4,1)S(1)}, u32[]{:S(2)}) copy-start(pred[128]{0:T(512)(128)(4,1)S(1)} %add_compare_fusion) | copy-start | bytes 388
  256.6 187.8 %all-to-all-start = ((bf16[16,128,1,2048]{3,1,2,0:T(8,128)(2,1)}), bf16[16,128,1,2048]{3,1,2,0:T(8,128)(2,1)}, u32[]{:S(2)}, u32[]{:S(2)}) async-start(bf16[16,128,1,2048]{3,1,2,0:T(8,128)(2,1)} %stack.16), calls=%async_computation.2 | async-start | bytes 16777216 | tf_op jit(solution)/shard_map/all_to_all | solution.py:203
  261.9 182.5 %copy-start.64 = (f32[512]{0:T(512)S(1)}, f32[512]{0:T(512)}, u32[]{:S(2)}) copy-start(f32[512]{0:T(512)} %param.27) | copy-start | bytes 6148
  261.9 317.5 %reduce-scatter.16.cloned.1.call-start = ((), (), s32[]{:S(2)}) async-start(), calls=%async_computation.14 | async-start | bytes 17825792 | tf_op jit(solution)/shard_map/reduce_scatter | solution.py:220
  444.4 13.8 copy-start.63
  466.5 200.8 %reduce-scatter.14.cloned.1.call-start = ((), (), s32[]{:S(2)}) async-start(), calls=%async_computation.13 | async-start | bytes 8912896 | tf_op jit(solution)/shard_map/reduce_scatter | solution.py:188
  476.6 190.6 %copy-start.49 = (f32[2048]{0:T(1024)S(1)}, f32[2048]{0:T(1024)}, u32[]{:S(2)}) copy-start(f32[2048]{0:T(1024)} %param.29) | copy-start | bytes 24580
  476.7 193.2 %copy-start.15 = (bf16[128,1,2048]{2,0,1:T(8,128)(2,1)S(1)}, bf16[128,1,2048]{2,0,1:T(8,128)(2,1)}, u32[]{:S(2)}) copy-start(bf16[128,1,2048]{2,0,1:T(8,128)(2,1)} %param.16) | copy-start | bytes 1572868
  476.7 265.1 %all-gather.8.cloned.1.call-start = ((), (), s32[]{:S(2)}) async-start(), calls=%async_computation.15 | async-start | bytes 8912896 | tf_op jit(solution)/shard_map/all_gather | solution.py:232
  671.6 219.1 %reduce-scatter.18.cloned.1.call-start = ((), (), s32[]{:S(2)}) async-start(), calls=%async_computation.16 | async-start | bytes 8912896 | tf_op jit(solution)/shard_map/reduce_scatter | solution.py:252
  676.2 81.5 %copy-start.38 = (f32[512]{0:T(512)}, f32[512]{0:T(512)S(1)}, u32[]{:S(2)}) copy-start(f32[512]{0:T(512)S(1)} %get-tuple-element.150) | copy-start | bytes 6148
  676.2 81.5 %copy-start.40 = (f32[512]{0:T(512)}, f32[512]{0:T(512)S(1)}, u32[]{:S(2)}) copy-start(f32[512]{0:T(512)S(1)} %get-tuple-element.149) | copy-start | bytes 6148
  676.8 65.0 %copy-start.30 = (bf16[1,128,2048]{2,1,0:T(8,128)(2,1)S(1)}, bf16[1,128,2048]{2,1,0:T(8,128)(2,1)}, u32[]{:S(2)}) copy-start(bf16[1,128,2048]{2,1,0:T(8,128)(2,1)} %param.22) | copy-start | bytes 1572868
  678.9 78.8 %copy-start.42 = (f32[512]{0:T(512)}, f32[512]{0:T(512)S(1)}, u32[]{:S(2)}) copy-start(f32[512]{0:T(512)S(1)} %get-tuple-element.151) | copy-start | bytes 6148
  678.9 78.8 %copy-start.44 = (f32[512]{0:T(512)}, f32[512]{0:T(512)S(1)}, u32[]{:S(2)}) copy-start(f32[512]{0:T(512)S(1)} %get-tuple-element.152) | copy-start | bytes 6148
  769.7 11.5 copy-start.18
  805.7 177.5 %reduce-scatter.26.cloned.1.call-start = ((), (), s32[]{:S(2)}) async-start(), calls=%async_computation.20 | async-start | bytes 2359296 | tf_op jit(solution)/shard_map/reduce_scatter | solution.py:279
  820.4 10.3 copy-start.20
  820.4 10.3 copy-start.22
  820.4 10.3 copy-start.24
  820.4 192.2 %reduce-scatter.24.cloned.1.call-start = ((), (), s32[]{:S(2)}) async-start(), calls=%async_computation.19 | async-start | bytes 2359296 | tf_op jit(solution)/shard_map/reduce_scatter | solution.py:276
  830.6 222.5 %reduce-scatter.22.cloned.1.call-start = ((), (), s32[]{:S(2)}) async-start(), calls=%async_computation.18 | async-start | bytes 589824 | tf_op jit(solution)/shard_map/reduce_scatter | solution.py:273
  836.3 54.4 %copy-start.10 = (bf16[128,1,2048]{2,0,1:T(8,128)(2,1)S(1)}, bf16[128,1,2048]{2,0,1:T(8,128)(2,1)}, u32[]{:S(2)}) copy-start(bf16[128,1,2048]{2,0,1:T(8,128)(2,1)} %param.15) | copy-start | bytes 1572868
  836.3 54.4 %copy-start.31 = (f32[2048]{0:T(1024)S(1)}, f32[2048]{0:T(1024)}, u32[]{:S(2)}) copy-start(f32[2048]{0:T(1024)} %param.18) | copy-start | bytes 24580
  836.3 54.4 %copy-start.46 = (f32[128]{0:T(128)S(1)}, f32[128]{0:T(128)}, u32[]{:S(2)}) copy-start(f32[128]{0:T(128)} %copy-done.45) | copy-start | bytes 1540
  836.3 55.9 %copy-start.62 = (f32[128]{0:T(128)S(1)}, f32[128]{0:T(128)}, u32[]{:S(2)}) copy-start(f32[128]{0:T(128)} %copy-done.61) | copy-start | bytes 1540
  836.3 55.9 %copy-start.52 = (f32[128]{0:T(128)S(1)}, f32[128]{0:T(128)}, u32[]{:S(2)}) copy-start(f32[128]{0:T(128)} %copy-done.51) | copy-start | bytes 1540
  836.3 264.1 %reduce-scatter.20.cloned.1.call-start = ((), (), s32[]{:S(2)}) async-start(), calls=%async_computation.17 | async-start | bytes 1769472 | tf_op jit(solution)/shard_map/reduce_scatter | solution.py:270
  845.0 49.0 %copy-start.16 = (bf16[128,1,2048]{2,0,1:T(8,128)(2,1)S(1)}, bf16[128,1,2048]{2,0,1:T(8,128)(2,1)}, u32[]{:S(2)}) copy-start(bf16[128,1,2048]{2,0,1:T(8,128)(2,1)} %param.16) | copy-start | bytes 1572868
  845.0 49.0 %copy-start.54 = (pred[128]{0:T(512)(128)(4,1)S(1)}, pred[128]{0:T(512)(128)(4,1)}, u32[]{:S(2)}) copy-start(pred[128]{0:T(512)(128)(4,1)} %copy-done.53) | copy-start | bytes 388
  845.0 49.0 %copy-start.57 = (f32[128]{0:T(128)S(1)}, f32[128]{0:T(128)}, u32[]{:S(2)}) copy-start(f32[128]{0:T(128)} %copy-done.56) | copy-start | bytes 1540
  845.0 51.8 %copy-start.33 = (f32[2048]{0:T(1024)S(1)}, f32[2048]{0:T(1024)}, u32[]{:S(2)}) copy-start(f32[2048]{0:T(1024)} %get-tuple-element.120) | copy-start | bytes 24580
  845.0 973.4 %reduce-scatter.28.cloned.1.call-start = ((), (), s32[]{:S(2)}) async-start(), calls=%async_computation.21 | async-start | bytes 1056768
  892.2 932.1 %copy-start.1 = (bf16[512,2048]{1,0:T(8,128)(2,1)S(1)}, bf16[512,2048]{1,0:T(8,128)(2,1)}, u32[]{:S(2)}) copy-start(bf16[512,2048]{1,0:T(8,128)(2,1)} %param.28) | copy-start | bytes 6291460
  (33 other events, 140.5 us)
Sparse Core Ops, SparseCore 0:
  12.9 71.8 all-gather.3
  137.4 110.1 reduce-scatter.11
  250.6 183.1 all-gather.5
  466.6 112.7 reduce-scatter.15
  582.6 84.6 reduce-scatter.13
  671.7 70.0 all-gather.7
  805.8 84.8 reduce-scatter.17
  893.1 55.0 reduce-scatter.25
  950.6 61.8 reduce-scatter.23
  1014.8 38.2 reduce-scatter.21
  1055.6 44.7 reduce-scatter.19
  1102.8 715.5 reduce-scatter.27
